TPU v7x, 128 devices: a whole 4x4x4 slice. The times are simulated.
128 devices in a mesh: row: 8 (over y, core), col: 16 (over z, x).
Axes of the slice: x: 4, y: 4, z: 4, core: 2. Of those that a mesh axis runs over, the one named last changes fastest.
Arguments:
- kernel_panel: float32 [64, 32768], P(None, ('row', 'col')), may hold values from -4 to 16, as said below
- kernel_slab: float32 [32768, 4096], P('row', 'col'), may hold values from -4 to 20, as said below
- targets: float32 [256, 32768], P(None, ('row', 'col')), may hold values from -6 to 6
Outputs:
- updated_slab: float32 [32768, 4096], P('row', 'col')
- solved_targets: float32 [256, 32768], P('col', 'row')
- panel_factor: float32 [64, 32768], P(None, ('row', 'col'))
Inputs may be any that keep to these rules, and one draw needn't show every extreme that they name: kernel_panel[:, 0:64] is symmetric and positive definite. `kernel_slab`: rows 0 to 63 equal kernel_panel[:, 32768 - 4096 : 32768]; the last 4096 rows form a symmetric matrix.
All inputs are finite; a program needn't handle non-finite values.
Results may differ from a plain program's by a relative error of at most 0.00018.
Values sent between devices are 32-bit elements; how exact they have to be, the bound alone decides.
No kernel may reach another device: no remote copies, remote signals or barrier semaphores. Data moves between devices by JAX's collectives and lax.ppermute only.
A program may use at most 64 MiB of HBM per device.

v0:
```python
import jax
import jax.numpy as jnp
from jax import lax
from jax.sharding import PartitionSpec as P


def spread(block, axis, source):
    block = jnp.where(lax.axis_index(axis) == source, block, jnp.zeros_like(block))
    return lax.psum(block, axis)


def lower_solve(factor, values):
    return jax.scipy.linalg.solve_triangular(factor, values, lower=True)


def body(kernel_panel, kernel_slab, targets):
    highest = lax.Precision.HIGHEST
    panel_width = kernel_panel.shape[0]
    row_count = lax.axis_size("row")
    row_index = lax.axis_index("row")
    flat_index = lax.axis_index(("row", "col"))
    corner_rows = jnp.concatenate([kernel_panel[:, :panel_width], targets[:, :panel_width]], 0)
    shared = spread(corner_rows, ("row", "col"), 0)
    lower_factor = jnp.linalg.cholesky(shared[:panel_width])
    panel_factor = lower_solve(lower_factor, kernel_panel)
    gathered = lax.all_gather(panel_factor, "col", axis=1, tiled=True)
    slab_factor = spread(panel_factor, "row", row_count - 1)
    product = lax.dot_general(
        gathered,
        slab_factor,
        (((0,), (0,)), ((), ())),
        precision=highest,
        preferred_element_type=jnp.float32,
    )
    update = kernel_slab - product
    head_rows = jnp.where(row_index == 0, slab_factor, update[:panel_width])
    updated_slab = jnp.concatenate([head_rows, update[panel_width:]], 0)
    solved_lead = lower_solve(lower_factor, shared[panel_width:].T).T
    result = targets - jnp.dot(
        solved_lead, panel_factor, precision=highest, preferred_element_type=jnp.float32
    )
    head_cols = jnp.where(flat_index == 0, solved_lead, result[:, :panel_width])
    result = jnp.concatenate([head_cols, result[:, panel_width:]], 1)
    solved_targets = lax.all_to_all(result, "col", split_axis=0, concat_axis=1, tiled=True)
    return (updated_slab, solved_targets, panel_factor)


def solution(mesh):
    in_specs = (P(None, ("row", "col")), P("row", "col"), P(None, ("row", "col")))
    out_specs = (P("row", "col"), P("col", "row"), P(None, ("row", "col")))
    return jax.shard_map(body, mesh=mesh, in_specs=in_specs, out_specs=out_specs, check_vma=False)
```

profile of v0, /device:TPU:0, one launch (start us, length us, event | category | flops | bytes accessed | tf_op | source)
XLA Modules:
  0.0 286.8 jit_solution(15664791899250229156)
XLA Ops:
  7.2 0.8 slice.34
  8.1 1.1 copy.17
  9.2 0.7 maximum_select_fusion
  10.0 143.3 %all-reduce.3.cloned.1.call-done = f32[320,64]{0,1:T(8,128)} async-done(((f32[320,64]{0,1:T(8,128)}), f32[320,64]{0,1:T(8,128)}) %all-reduce.3.cloned.1.call-update) | async-done | bytes 81936 | tf_op jit(solution)/shard_map/psum | solution.py:9
  153.3 0.8 slice.43
  154.1 0.8 fusion.5
  154.9 5.8 %cholesky.18 = f32[64,64]{1,0:T(8,128)S(1)} custom-call(f32[64,64]{1,0:T(8,128)S(1)} %fusion.5), custom_call_target="Cholesky" | custom-call | tf_op jit(solution)/shard_map/jit(cholesky)/cholesky | solution.py:24
  160.8 0.6 compare_reduce_fusion
  161.4 0.7 fusion.1
  162.1 4.9 %custom-call.7 = f32[1,64,64]{1,2,0:T(8,128)S(1)} custom-call(f32[1,64,64]{2,1,0:T(8,128)S(1)} %fusion.1), custom_call_target="InvertDiagBlocksLowerTriangular" | custom-call | tf_op jit(solution)/shard_map/jit(_solve_triangular)/triangular_solve | solution.py:13
  167.0 1.8 broadcast_select_fusion
  168.8 0.7 all-gather.2.cloned.1.call-update
  169.5 1.2 fusion
  170.7 1.3 convolution_subtract_fusion.1
  172.0 0.8 copy.20
  172.9 5.6 %all-to-all-start = ((f32[16,16,256]{2,1,0:T(8,128)}), f32[16,16,256]{2,1,0:T(8,128)S(1)}, u32[]{:S(2)}, u32[]{:S(2)}) async-start(f32[16,16,256]{2,1,0:T(8,128)} %bitcast.7), calls=%async_computation | async-start | bytes 524288 | tf_op jit(solution)/shard_map/all_to_all | solution.py:44
  178.5 8.7 %all-to-all-done = f32[16,16,256]{2,1,0:T(8,128)S(1)} async-done(((f32[16,16,256]{2,1,0:T(8,128)}), f32[16,16,256]{2,1,0:T(8,128)S(1)}, u32[]{:S(2)}, u32[]{:S(2)}) %all-to-all-start) | async-done | bytes 262176 | tf_op jit(solution)/shard_map/all_to_all | solution.py:44
  187.2 0.7 copy.23
  187.9 38.0 %all-reduce.5.cloned.1.call-done = f32[64,256]{1,0:T(8,128)} async-done(((f32[64,256]{1,0:T(8,128)}), f32[64,256]{1,0:T(8,128)}) %all-reduce.5.cloned.1.call-update) | async-done | bytes 65552 | tf_op jit(solution)/shard_map/psum | solution.py:9
  225.9 45.2 %all-gather.2.cloned.1.call-done = f32[64,4096]{1,0:T(8,128)} async-done(((f32[64,256]{1,0:T(8,128)}), f32[64,4096]{1,0:T(8,128)}) %all-gather.2.cloned.1.call-update) | async-done | bytes 1048592 | tf_op jit(solution)/shard_map/all_gather | solution.py:26
  271.1 6.0 %convolution_subtract_fusion = f32[4096,256]{1,0:T(8,128)S(1)} fusion(f32[4096,256]{1,0:T(8,128)} %param.6, f32[64,4096]{1,0:T(8,128)} %all-gather.2.cloned.1.call-done, f32[64,256]{1,0:T(8,128)} %all-reduce.5.cloned.1.call-done), kind=kOutput, calls=%fused_computation | convolution fusion | flops 806354944 | bytes 9502720 | tf_op jit(solution)/shard_map/dot_general | solution.py:28
  277.1 0.3 slice.45
  277.4 0.6 copy-done
  278.0 2.3 pad_maximum_fusion
  (14 shorter events, 0.4 us)
Async XLA Ops:
  7.2 146.1 %all-reduce.3.cloned.1.call-start = ((), (), s32[]{:S(2)}) async-start(), calls=%async_computation.1 | async-start | bytes 196608 | tf_op jit(solution)/shard_map/psum | solution.py:9
  9.9 216.0 %all-reduce.5.cloned.1.call-start = ((), (), s32[]{:S(2)}) async-start(), calls=%async_computation.2 | async-start | bytes 131072 | tf_op jit(solution)/shard_map/psum | solution.py:9
  168.8 102.3 %all-gather.2.cloned.1.call-start = ((), (), s32[]{:S(2)}) async-start(), calls=%async_computation.3 | async-start | bytes 1114112 | tf_op jit(solution)/shard_map/all_gather | solution.py:26
  172.9 14.3 %all-to-all-start = ((f32[16,16,256]{2,1,0:T(8,128)}), f32[16,16,256]{2,1,0:T(8,128)S(1)}, u32[]{:S(2)}, u32[]{:S(2)}) async-start(f32[16,16,256]{2,1,0:T(8,128)} %bitcast.7), calls=%async_computation | async-start | bytes 524288 | tf_op jit(solution)/shard_map/all_to_all | solution.py:44
  277.1 0.8 copy-start
Sparse Core Ops, SparseCore 0:
  13.3 139.9 all-reduce.2
  168.9 56.9 all-reduce.4
  228.6 42.4 all-gather.1
where the time goes:
time: 287 us
  waiting for transfers between devices  236 us (82%)
  other arithmetic  15.9 us (6%)
  between operations  13.9 us (5%)
  matrix products  10.2 us (4%)
  starting transfers between devices  5.75 us (2%)
  local copies, waits for them, and re-layouts  5.16 us (2%)
    psum x2, waiting for transfers between devices, spread(): return lax.psum(block, axis)  181 us
    all_gather x1, waiting for transfers between devices, body(): gathered = lax.all_gather(panel_factor, 'col', axis=1, tiled=True)  45.2 us
    all_to_all x1, waiting for transfers between devices, body(): lax.all_to_all(result, 'col', split_axis=0, concat_axis=1, tiled=True)  8.69 us
    another operation x3, other arithmetic, body(): lower_factor = jnp.linalg.cholesky(shared[:panel_width])  6.52 us
    dot_general x1, matrix products, body(): lax.dot_general(gathered, slab_factor, (((0,), (0,)), ((), ())), precisio...  6 us
  transfers between devices with their start and end apart: 4, of which 4 were waited for; matrix products, arithmetic and copies ran while one was open for 1% of the time, Pallas kernels for 0%

commit v1 on v0

--- a/solution.py
+++ b/solution.py
@@ -2,6 +2,31 @@
 import jax.numpy as jnp
 from jax import lax
 from jax.sharding import PartitionSpec as P
+
+
+def answer_points(arr_in):
+    r_now, a_next, all_rows = (lax.axis_size("col"), lax.axis_index("col"), arr_in.shape[1])
+    table = []
+    for i in range(r_now):
+        table.append((i, (i + 1) % r_now))
+    log = []
+    for i in range(r_now):
+        log.append((i, (i - 1) % r_now))
+    z_new = jnp.zeros((*arr_in.shape[:1], r_now * all_rows, *arr_in.shape[2:]), arr_in.dtype)
+    z_new = lax.dynamic_update_slice_in_dim(z_new, arr_in, a_next * all_rows, axis=1)
+    prior = field_out = arr_in
+    taken_in = r_now // 2
+    for ix in range(1, taken_in + 1):
+        prior = lax.ppermute(prior, perm=table, axis_name="col")
+        z_new = lax.dynamic_update_slice_in_dim(
+            z_new, prior, (a_next - ix) % r_now * all_rows, axis=1
+        )
+        if ix < r_now - taken_in:
+            field_out = lax.ppermute(field_out, axis_name="col", perm=log)
+            z_new = lax.dynamic_update_slice_in_dim(
+                z_new, field_out, (a_next + ix) % r_now * all_rows, axis=1
+            )
+    return z_new
 
 
 def spread(block, axis, source):
@@ -23,7 +48,7 @@
     shared = spread(corner_rows, ("row", "col"), 0)
     lower_factor = jnp.linalg.cholesky(shared[:panel_width])
     panel_factor = lower_solve(lower_factor, kernel_panel)
-    gathered = lax.all_gather(panel_factor, "col", axis=1, tiled=True)
+    gathered = answer_points(panel_factor)
     slab_factor = spread(panel_factor, "row", row_count - 1)
     product = lax.dot_general(
         gathered,

time: 287 us -> 256 us (0.89)
  waiting for transfers between devices: 236 us -> 167 us
  starting transfers between devices: 5.75 us -> 43.9 us
    all_gather x1 -> x0, waiting for transfers between devices: 45.2 us -> none  [body(): gathered = lax.all_gather(panel_factor, 'col', axis=1, tiled=True)]
    psum x2, waiting for transfers between devices: 181 us -> 143 us  [spread(): return lax.psum(block, axis)]
    ppermute x0 -> x15, starting transfers between devices: none -> 37.1 us  [the longest x7 37 us: answer_points(): field_out = lax.ppermute(field_out, axis_name='col', perm=log)]
    ppermute x0 -> x15, waiting for transfers between devices: none -> 23.9 us  [the longest x8 15.4 us: answer_points(): prior = lax.ppermute(prior, perm=table, axis_name='col')]
    all_to_all x1, waiting for transfers between devices: 8.69 us -> 0.01 us  [body(): lax.all_to_all(result, 'col', split_axis=0, concat_axis=1, tiled=True)]
  transfers between devices with their start and end apart: 4 -> 18, of which waited for: 4 -> 9; matrix products, arithmetic and copies ran while one was open for 1% -> 1% of each run, Pallas kernels for 0% -> 0%
where the time goes in v1:
time: 256 us; the launch traced here: 255 us
  waiting for transfers between devices  167 us (65%)
  starting transfers between devices  43.9 us (17%)
  other arithmetic  15.9 us (6%)
  between operations  14.6 us (6%)
  matrix products  8.68 us (3%)
  local copies, waits for them, and re-layouts  5.4 us (2%)
    psum x2, waiting for transfers between devices, spread(): return lax.psum(block, axis)  143 us
    ppermute x7, starting transfers between devices, answer_points(): field_out = lax.ppermute(field_out, axis_name='col', perm=log)  37 us
    ppermute x8, waiting for transfers between devices, answer_points(): prior = lax.ppermute(prior, perm=table, axis_name='col')  15.4 us
    ppermute x7, waiting for transfers between devices, answer_points(): field_out = lax.ppermute(field_out, axis_name='col', perm=log)  8.59 us
    all_to_all x1, starting transfers between devices, body(): lax.all_to_all(result, 'col', split_axis=0, concat_axis=1, tiled=True)  6.74 us
    another operation x3, other arithmetic, body(): lower_factor = jnp.linalg.cholesky(shared[:panel_width])  6.52 us
    another operation x2, other arithmetic, lower_solve(): return jax.scipy.linalg.solve_triangular(factor, values, lower=True)  5.55 us
    dot_general x1, matrix products, body(): lax.dot_general(gathered, slab_factor, (((0,), (0,)), ((), ())), precisio...  5.32 us
  transfers between devices with their start and end apart: 18, of which 9 were waited for; matrix products, arithmetic and copies ran while one was open for 1% of the time, Pallas kernels for 0%

profile of v1, /device:TPU:0, one launch (start us, length us, event | category | flops | bytes accessed | tf_op | source)
XLA Modules:
  0.0 255.5 jit_solution(16245997599633159891)
XLA Ops:
  8.1 1.1 copy.17
  10.3 143.0 %all-reduce.3.cloned.1.call-done = f32[320,64]{0,1:T(8,128)} async-done(((f32[320,64]{0,1:T(8,128)}), f32[320,64]{0,1:T(8,128)}) %all-reduce.3.cloned.1.call-update) | async-done | bytes 81936 | tf_op jit(solution)/shard_map/psum | solution.py:34
  154.9 5.8 %cholesky.18 = f32[64,64]{1,0:T(8,128)S(1)} custom-call(f32[64,64]{1,0:T(8,128)S(1)} %fusion.5), custom_call_target="Cholesky" | custom-call | tf_op jit(solution)/shard_map/jit(cholesky)/cholesky | solution.py:49
  162.1 4.9 %custom-call.7 = f32[1,64,64]{1,2,0:T(8,128)S(1)} custom-call(f32[1,64,64]{2,1,0:T(8,128)S(1)} %fusion.1), custom_call_target="InvertDiagBlocksLowerTriangular" | custom-call | tf_op jit(solution)/shard_map/jit(_solve_triangular)/triangular_solve | solution.py:38
  167.1 1.7 broadcast_select_fusion
  168.8 1.2 fusion
  170.5 3.2 %collective-permute-start.1 = (f32[64,256]{1,0:T(8,128)S(1)}, f32[64,256]{1,0:T(8,128)S(1)}, u32[]{:S(2)}, u32[]{:S(2)}) collective-permute-start(f32[64,256]{1,0:T(8,128)S(1)} %get-tuple-element.6), channel_id=1, source_target_pairs={{0,15},{1,0},{2,1},{3,2},{4,3},{5,4},{6,5},{7,6},{8,7},{9,8},{10,9... | collective-permute-start | bytes 196616 | tf_op jit(solution)/shard_map/ppermute | solution.py:25
  173.7 0.8 copy.20
  174.6 6.7 %all-to-all-start = ((f32[16,16,256]{2,1,0:T(8,128)}), f32[16,16,256]{2,1,0:T(8,128)S(1)}, u32[]{:S(2)}, u32[]{:S(2)}) async-start(f32[16,16,256]{2,1,0:T(8,128)} %bitcast.7), calls=%async_computation | async-start | bytes 524288 | tf_op jit(solution)/shard_map/all_to_all | solution.py:69
  181.3 5.3 %collective-permute-start.3 = (f32[64,256]{1,0:T(8,128)S(1)}, f32[64,256]{1,0:T(8,128)S(1)}, u32[]{:S(2)}, u32[]{:S(2)}) collective-permute-start(f32[64,256]{1,0:T(8,128)S(1)} %collective-permute-done.1), channel_id=1, source_target_pairs={{0,15},{1,0},{2,1},{3,2},{4,3},{5,4},{6,5},{7,6},{8,7},{9,8},{10,9... | collective-permute-start | bytes 196616 | tf_op jit(solution)/shard_map/ppermute | solution.py:25
  186.7 1.9 collective-permute-done.3
  188.6 5.7 %collective-permute-start.5 = (f32[64,256]{1,0:T(8,128)S(1)}, f32[64,256]{1,0:T(8,128)S(1)}, u32[]{:S(2)}, u32[]{:S(2)}) collective-permute-start(f32[64,256]{1,0:T(8,128)S(1)} %collective-permute-done.3), channel_id=1, source_target_pairs={{0,15},{1,0},{2,1},{3,2},{4,3},{5,4},{6,5},{7,6},{8,7},{9,8},{10,9... | collective-permute-start | bytes 196616 | tf_op jit(solution)/shard_map/ppermute | solution.py:25
  194.3 1.9 collective-permute-done.5
  196.1 5.7 %collective-permute-start.7 = (f32[64,256]{1,0:T(8,128)S(1)}, f32[64,256]{1,0:T(8,128)S(1)}, u32[]{:S(2)}, u32[]{:S(2)}) collective-permute-start(f32[64,256]{1,0:T(8,128)S(1)} %collective-permute-done.5), channel_id=1, source_target_pairs={{0,15},{1,0},{2,1},{3,2},{4,3},{5,4},{6,5},{7,6},{8,7},{9,8},{10,9... | collective-permute-start | bytes 196616 | tf_op jit(solution)/shard_map/ppermute | solution.py:25
  202.6 1.1 collective-permute-done.7
  203.7 5.7 %collective-permute-start.9 = (f32[64,256]{1,0:T(8,128)S(1)}, f32[64,256]{1,0:T(8,128)S(1)}, u32[]{:S(2)}, u32[]{:S(2)}) collective-permute-start(f32[64,256]{1,0:T(8,128)S(1)} %collective-permute-done.7), channel_id=1, source_target_pairs={{0,15},{1,0},{2,1},{3,2},{4,3},{5,4},{6,5},{7,6},{8,7},{9,8},{10,9... | collective-permute-start | bytes 196616 | tf_op jit(solution)/shard_map/ppermute | solution.py:25
  209.5 1.9 collective-permute-done.9
  211.3 5.7 %collective-permute-start.11 = (f32[64,256]{1,0:T(8,128)S(1)}, f32[64,256]{1,0:T(8,128)S(1)}, u32[]{:S(2)}, u32[]{:S(2)}) collective-permute-start(f32[64,256]{1,0:T(8,128)S(1)} %collective-permute-done.9), channel_id=1, source_target_pairs={{0,15},{1,0},{2,1},{3,2},{4,3},{5,4},{6,5},{7,6},{8,7},{9,8},{10,9... | collective-permute-start | bytes 196616 | tf_op jit(solution)/shard_map/ppermute | solution.py:25
  217.3 1.8 collective-permute-done.11
  219.1 5.8 %collective-permute-start.13 = (f32[64,256]{1,0:T(8,128)S(1)}, f32[64,256]{1,0:T(8,128)S(1)}, u32[]{:S(2)}, u32[]{:S(2)}) collective-permute-start(f32[64,256]{1,0:T(8,128)S(1)} %collective-permute-done.11), channel_id=1, source_target_pairs={{0,15},{1,0},{2,1},{3,2},{4,3},{5,4},{6,5},{7,6},{8,7},{9,8},{10,9... | collective-permute-start | bytes 196616 | tf_op jit(solution)/shard_map/ppermute | solution.py:25
  225.0 7.5 %collective-permute-done.12 = f32[64,256]{1,0:T(8,128)S(1)} collective-permute-done((f32[64,256]{1,0:T(8,128)S(1)}, f32[64,256]{1,0:T(8,128)S(1)}, u32[]{:S(2)}, u32[]{:S(2)}) %collective-permute-start.12) | collective-permute-done | bytes 65568 | tf_op jit(solution)/shard_map/ppermute | solution.py:20
  232.6 7.5 %collective-permute-done.14 = f32[64,256]{1,0:T(8,128)S(1)} collective-permute-done((f32[64,256]{1,0:T(8,128)S(1)}, f32[64,256]{1,0:T(8,128)S(1)}, u32[]{:S(2)}, u32[]{:S(2)}) %collective-permute-start.14) | collective-permute-done | bytes 65568 | tf_op jit(solution)/shard_map/ppermute | solution.py:20
  240.2 5.3 %convolution_subtract_fusion = f32[4096,256]{1,0:T(8,128)S(1)} fusion(f32[4096,256]{1,0:T(8,128)} %param.6, f32[64,4096]{1,0:T(8,128)S(1)} %constant_dynamic-update-slice_fusion, f32[64,256]{1,0:T(8,128)} %all-reduce.5.cloned.1.call-done), kind=kOutput, calls=%fused_computation | convolution fusion | flops 806354944 | bytes 9502720 | tf_op jit(solution)/shard_map/dot_general | solution.py:53
  246.3 2.3 pad_maximum_fusion
  (59 shorter events, 7.2 us)
Async XLA Ops:
  7.2 146.1 %all-reduce.3.cloned.1.call-start = ((), (), s32[]{:S(2)}) async-start(), calls=%async_computation.1 | async-start | bytes 196608 | tf_op jit(solution)/shard_map/psum | solution.py:34
  9.9 230.2 %all-reduce.5.cloned.1.call-start = ((), (), s32[]{:S(2)}) async-start(), calls=%async_computation.2 | async-start | bytes 131072 | tf_op jit(solution)/shard_map/psum | solution.py:34
  168.8 76.7 %copy-start.1 = (f32[64,256]{1,0:T(8,128)}, f32[64,256]{1,0:T(8,128)S(1)}, u32[]{:S(2)}) copy-start(f32[64,256]{1,0:T(8,128)S(1)} %get-tuple-element.6) | copy-start | bytes 196612
  170.5 10.8 %collective-permute-start.1 = (f32[64,256]{1,0:T(8,128)S(1)}, f32[64,256]{1,0:T(8,128)S(1)}, u32[]{:S(2)}, u32[]{:S(2)}) collective-permute-start(f32[64,256]{1,0:T(8,128)S(1)} %get-tuple-element.6), channel_id=1, source_target_pairs={{0,15},{1,0},{2,1},{3,2},{4,3},{5,4},{6,5},{7,6},{8,7},{9,8},{10,9... | collective-permute-start | bytes 196616 | tf_op jit(solution)/shard_map/ppermute | solution.py:25
  173.7 13.0 %collective-permute-start = (f32[64,256]{1,0:T(8,128)S(1)}, f32[64,256]{1,0:T(8,128)S(1)}, u32[]{:S(2)}, u32[]{:S(2)}) collective-permute-start(f32[64,256]{1,0:T(8,128)S(1)} %get-tuple-element.6), channel_id=1, source_target_pairs={{0,1},{1,2},{2,3},{3,4},{4,5},{5,6},{6,7},{7,8},{8,9},{9,10},{10,1... | collective-permute-start | bytes 196616 | tf_op jit(solution)/shard_map/ppermute | solution.py:20
  174.6 27.3 %all-to-all-start = ((f32[16,16,256]{2,1,0:T(8,128)}), f32[16,16,256]{2,1,0:T(8,128)S(1)}, u32[]{:S(2)}, u32[]{:S(2)}) async-start(f32[16,16,256]{2,1,0:T(8,128)} %bitcast.7), calls=%async_computation | async-start | bytes 524288 | tf_op jit(solution)/shard_map/all_to_all | solution.py:69
  181.3 7.2 %collective-permute-start.3 = (f32[64,256]{1,0:T(8,128)S(1)}, f32[64,256]{1,0:T(8,128)S(1)}, u32[]{:S(2)}, u32[]{:S(2)}) collective-permute-start(f32[64,256]{1,0:T(8,128)S(1)} %collective-permute-done.1), channel_id=1, source_target_pairs={{0,15},{1,0},{2,1},{3,2},{4,3},{5,4},{6,5},{7,6},{8,7},{9,8},{10,9... | collective-permute-start | bytes 196616 | tf_op jit(solution)/shard_map/ppermute | solution.py:25
  186.7 7.6 %collective-permute-start.2 = (f32[64,256]{1,0:T(8,128)S(1)}, f32[64,256]{1,0:T(8,128)S(1)}, u32[]{:S(2)}, u32[]{:S(2)}) collective-permute-start(f32[64,256]{1,0:T(8,128)S(1)} %collective-permute-done), channel_id=1, source_target_pairs={{0,1},{1,2},{2,3},{3,4},{4,5},{5,6},{6,7},{7,8},{8,9},{9,10},{10,1... | collective-permute-start | bytes 196616 | tf_op jit(solution)/shard_map/ppermute | solution.py:20
  188.6 7.6 %collective-permute-start.5 = (f32[64,256]{1,0:T(8,128)S(1)}, f32[64,256]{1,0:T(8,128)S(1)}, u32[]{:S(2)}, u32[]{:S(2)}) collective-permute-start(f32[64,256]{1,0:T(8,128)S(1)} %collective-permute-done.3), channel_id=1, source_target_pairs={{0,15},{1,0},{2,1},{3,2},{4,3},{5,4},{6,5},{7,6},{8,7},{9,8},{10,9... | collective-permute-start | bytes 196616 | tf_op jit(solution)/shard_map/ppermute | solution.py:25
  194.2 7.6 %collective-permute-start.4 = (f32[64,256]{1,0:T(8,128)S(1)}, f32[64,256]{1,0:T(8,128)S(1)}, u32[]{:S(2)}, u32[]{:S(2)}) collective-permute-start(f32[64,256]{1,0:T(8,128)S(1)} %collective-permute-done.2), channel_id=1, source_target_pairs={{0,1},{1,2},{2,3},{3,4},{4,5},{5,6},{6,7},{7,8},{8,9},{9,10},{10,1... | collective-permute-start | bytes 196616 | tf_op jit(solution)/shard_map/ppermute | solution.py:20
  196.1 7.6 %collective-permute-start.7 = (f32[64,256]{1,0:T(8,128)S(1)}, f32[64,256]{1,0:T(8,128)S(1)}, u32[]{:S(2)}, u32[]{:S(2)}) collective-permute-start(f32[64,256]{1,0:T(8,128)S(1)} %collective-permute-done.5), channel_id=1, source_target_pairs={{0,15},{1,0},{2,1},{3,2},{4,3},{5,4},{6,5},{7,6},{8,7},{9,8},{10,9... | collective-permute-start | bytes 196616 | tf_op jit(solution)/shard_map/ppermute | solution.py:25
  201.8 7.6 %collective-permute-start.6 = (f32[64,256]{1,0:T(8,128)S(1)}, f32[64,256]{1,0:T(8,128)S(1)}, u32[]{:S(2)}, u32[]{:S(2)}) collective-permute-start(f32[64,256]{1,0:T(8,128)S(1)} %collective-permute-done.4), channel_id=1, source_target_pairs={{0,1},{1,2},{2,3},{3,4},{4,5},{5,6},{6,7},{7,8},{8,9},{9,10},{10,1... | collective-permute-start | bytes 196616 | tf_op jit(solution)/shard_map/ppermute | solution.py:20
  203.7 7.6 %collective-permute-start.9 = (f32[64,256]{1,0:T(8,128)S(1)}, f32[64,256]{1,0:T(8,128)S(1)}, u32[]{:S(2)}, u32[]{:S(2)}) collective-permute-start(f32[64,256]{1,0:T(8,128)S(1)} %collective-permute-done.7), channel_id=1, source_target_pairs={{0,15},{1,0},{2,1},{3,2},{4,3},{5,4},{6,5},{7,6},{8,7},{9,8},{10,9... | collective-permute-start | bytes 196616 | tf_op jit(solution)/shard_map/ppermute | solution.py:25
  209.4 7.8 %collective-permute-start.8 = (f32[64,256]{1,0:T(8,128)S(1)}, f32[64,256]{1,0:T(8,128)S(1)}, u32[]{:S(2)}, u32[]{:S(2)}) collective-permute-start(f32[64,256]{1,0:T(8,128)S(1)} %collective-permute-done.6), channel_id=1, source_target_pairs={{0,1},{1,2},{2,3},{3,4},{4,5},{5,6},{6,7},{7,8},{8,9},{9,10},{10,1... | collective-permute-start | bytes 196616 | tf_op jit(solution)/shard_map/ppermute | solution.py:20
  211.3 7.8 %collective-permute-start.11 = (f32[64,256]{1,0:T(8,128)S(1)}, f32[64,256]{1,0:T(8,128)S(1)}, u32[]{:S(2)}, u32[]{:S(2)}) collective-permute-start(f32[64,256]{1,0:T(8,128)S(1)} %collective-permute-done.9), channel_id=1, source_target_pairs={{0,15},{1,0},{2,1},{3,2},{4,3},{5,4},{6,5},{7,6},{8,7},{9,8},{10,9... | collective-permute-start | bytes 196616 | tf_op jit(solution)/shard_map/ppermute | solution.py:25
  217.3 7.7 %collective-permute-start.10 = (f32[64,256]{1,0:T(8,128)S(1)}, f32[64,256]{1,0:T(8,128)S(1)}, u32[]{:S(2)}, u32[]{:S(2)}) collective-permute-start(f32[64,256]{1,0:T(8,128)S(1)} %collective-permute-done.8), channel_id=1, source_target_pairs={{0,1},{1,2},{2,3},{3,4},{4,5},{5,6},{6,7},{7,8},{8,9},{9,10},{10,1... | collective-permute-start | bytes 196616 | tf_op jit(solution)/shard_map/ppermute | solution.py:20
  219.1 13.4 %collective-permute-start.13 = (f32[64,256]{1,0:T(8,128)S(1)}, f32[64,256]{1,0:T(8,128)S(1)}, u32[]{:S(2)}, u32[]{:S(2)}) collective-permute-start(f32[64,256]{1,0:T(8,128)S(1)} %collective-permute-done.11), channel_id=1, source_target_pairs={{0,15},{1,0},{2,1},{3,2},{4,3},{5,4},{6,5},{7,6},{8,7},{9,8},{10,9... | collective-permute-start | bytes 196616 | tf_op jit(solution)/shard_map/ppermute | solution.py:25
  224.9 7.6 %collective-permute-start.12 = (f32[64,256]{1,0:T(8,128)S(1)}, f32[64,256]{1,0:T(8,128)S(1)}, u32[]{:S(2)}, u32[]{:S(2)}) collective-permute-start(f32[64,256]{1,0:T(8,128)S(1)} %collective-permute-done.10), channel_id=1, source_target_pairs={{0,1},{1,2},{2,3},{3,4},{4,5},{5,6},{6,7},{7,8},{8,9},{9,10},{10,1... | collective-permute-start | bytes 196616 | tf_op jit(solution)/shard_map/ppermute | solution.py:20
  232.5 7.6 %collective-permute-start.14 = (f32[64,256]{1,0:T(8,128)S(1)}, f32[64,256]{1,0:T(8,128)S(1)}, u32[]{:S(2)}, u32[]{:S(2)}) collective-permute-start(f32[64,256]{1,0:T(8,128)S(1)} %collective-permute-done.12), channel_id=1, source_target_pairs={{0,1},{1,2},{2,3},{3,4},{4,5},{5,6},{6,7},{7,8},{8,9},{9,10},{10,1... | collective-permute-start | bytes 196616 | tf_op jit(solution)/shard_map/ppermute | solution.py:20
  245.5 0.8 copy-start
Sparse Core Ops, SparseCore 0:
  13.3 139.9 all-reduce.2
  174.7 58.4 all-reduce.4
